TPU v7x, 32 devices: a whole 2x2x4 slice. The times are simulated.
32 devices in a mesh: pix: 4 (over z), mode: 8 (over y, x, core).
Axes of the slice: x: 2, y: 2, z: 4, core: 2. Of those that a mesh axis runs over, the one named last changes fastest.
Arguments:
- frames: float32 [4, 4096, 8192], P(None, 'pix', 'mode'), may hold values from 0 to 500, as said below
- phase_steps: int32 [4], replicated, may hold values from 0 to 3, each once
- pattern_rows: int32 [8192], replicated, may hold values from 0 to 8191, each once
- probes: float32 [2, 32, 8192], replicated, may hold values from -6 to 6
Outputs:
- channels: float32 [2, 32, 8192], replicated
- fields: float32 [2, 32, 4096], P(None, None, ('pix', 'mode'))
- strengths: float32 [32], replicated
Inputs may be any that keep to these rules, and one draw needn't show every extreme that they name: `phase_steps`: each frame has its own phase step. `pattern_rows`: every Hadamard row is displayed exactly once. `frames`: intensities are not negative.
All inputs are finite; a program needn't handle non-finite values.
Results may differ from a plain program's by a relative error of at most 0.0003.
Values sent between devices are 32-bit elements; how exact they have to be, the bound alone decides.
No kernel may reach another device: no remote copies, remote signals or barrier semaphores. Data moves between devices by JAX's collectives and lax.ppermute only.
A program may use at most 128 MiB of HBM per device.

v0:
```python
import math
import jax
import jax.numpy as jnp
from jax import lax
from jax.sharding import PartitionSpec as P

HB = 128
ITERS = 2
precise = lax.Precision.HIGHEST


def demodulate(frames, phase_steps):
    cosine = (phase_steps == 0).astype(jnp.float32) - (phase_steps == 2).astype(jnp.float32)
    sine_part = (phase_steps == 1).astype(jnp.float32) - (phase_steps == 3).astype(jnp.float32)
    real_part = cosine[0] * frames[0]
    imag_part = sine_part[0] * frames[0]
    for frame_index in range(1, frames.shape[0]):
        real_part = real_part + cosine[frame_index] * frames[frame_index]
        imag_part = imag_part + sine_part[frame_index] * frames[frame_index]
    return (0.25 * real_part, 0.25 * imag_part)


def sign_table(table_order):
    positions = jnp.arange(table_order, dtype=jnp.int32)
    common = positions[:, None] & positions[None, :]
    parity = jnp.zeros((table_order, table_order), jnp.int32)
    for bit_place in range(table_order.bit_length() - 1):
        parity = parity + (common >> bit_place & 1)
    return (1 - 2 * (parity & 1)).astype(jnp.float32)


def hadamard_rows(values):
    length = values.shape[-1]
    leading = values.shape[:-1]
    inner_signs = sign_table(HB)
    outer_signs = sign_table(length // HB)
    shaped = values.reshape((-1, length // HB, HB))
    shaped = jnp.matmul(shaped, inner_signs, precision=precise)
    shaped = jnp.einsum("ab,nbc->nac", outer_signs, shaped, precision=precise)
    return shaped.reshape(leading + (length,)) * (1.0 / math.sqrt(length))


def contract_last(first_arg, second_arg):
    return lax.dot_general(first_arg, second_arg, (((1,), (1,)), ((), ())), precision=precise)


def forward(matrix, vectors):
    real_out = contract_last(vectors[0], matrix[0]) - contract_last(vectors[1], matrix[1])
    imag_out = contract_last(vectors[1], matrix[0]) + contract_last(vectors[0], matrix[1])
    return jnp.stack([real_out, imag_out])


def backward(matrix, images):
    real_out = jnp.dot(images[0], matrix[0], precision=precise) + jnp.dot(
        images[1], matrix[1], precision=precise
    )
    imag_out = jnp.dot(images[1], matrix[0], precision=precise) - jnp.dot(
        images[0], matrix[1], precision=precise
    )
    return jnp.stack([real_out, imag_out])


def orthonormal(vectors):
    mode_count = vectors.shape[2]
    stacked = jnp.concatenate([vectors[0], vectors[1]], axis=1)
    gram_matrix = jnp.dot(stacked, stacked.T, precision=precise)
    factor = jnp.linalg.cholesky(gram_matrix)
    solved = lax.linalg.triangular_solve(factor, stacked, left_side=True, lower=True)
    return jnp.stack([solved[:, :mode_count], solved[:, mode_count:]])


def local(frames, phase_steps, pattern_rows, probes):
    columns = frames.shape[2]
    groups = lax.axis_size("mode")
    modes_total = columns * groups
    devices = lax.axis_size("pix") * groups
    real_part, imag_part = demodulate(frames, phase_steps)
    positions = jnp.arange(modes_total, dtype=jnp.int32)
    inverse = jnp.zeros((modes_total,), jnp.int32).at[pattern_rows].set(positions)
    current = orthonormal(probes)
    rows_here = real_part.shape[0] // groups
    demodulated = jnp.stack([real_part, imag_part]).reshape(2, groups, rows_here, columns)
    ordered = jnp.take(
        lax.all_to_all(demodulated, "mode", split_axis=1, concat_axis=3, tiled=True),
        inverse,
        axis=3,
    )
    matrix = hadamard_rows(ordered)
    matrix = matrix.reshape(2, rows_here, modes_total)
    for iteration in range(ITERS):
        images = forward(matrix, current)
        returned = lax.psum(backward(matrix, images), ("pix", "mode"))
        current = orthonormal(returned)
    fields = forward(matrix, current)
    local_power = jnp.sum(fields * fields, axis=(0, 2))
    strengths = lax.psum(local_power, ("pix", "mode")) / (fields.shape[2] * devices)
    channels = math.sqrt(modes_total) * current
    return (channels, fields, strengths)


def solution(mesh):
    in_specs = (P(None, "pix", "mode"), P(), P(), P())
    out_specs = (P(), P(None, None, ("pix", "mode")), P())
    return jax.shard_map(local, mesh=mesh, in_specs=in_specs, out_specs=out_specs, check_vma=False)
```

profile of v0, /device:TPU:0, one launch (start us, length us, event | category | flops | bytes accessed | tf_op | source)
XLA Modules:
  0.0 704.6 jit_solution(8088165573559418275)
XLA Ops:
  8.5 12.0 %add_multiply_fusion.1 = (f32[1,1024,1024]{2,1,0:T(8,128)S(1)}, f32[1,1024,1024]{2,1,0:T(8,128)S(1)}) fusion(f32[4,1024,1024]{2,1,0:T(8,128)} %param.7, f32[]{:T(128)} %bitcast.9, f32[]{:T(128)} %bitcast.8, f32[]{:T(128)} %bitcast.7, f32[]{:T(128)} %bitcast.6, f32[]{:T(128)} %bitcast.14, f32[]{:T(128)} %bitcast.13, f32[]{:T(128)} %bitcast.12, f32[]{:T(128)} %bitcast.11), kind=kLoop, calls=%fused_computation.52 | loop fusion | flops 16777216 | bytes 25165856 | tf_op jit(solution)/shard_map/mul | solution.py:20
  26.3 5.3 all-to-all-start
  41.4 30.7 %scatter_custom_fusion = s32[8192]{0:T(1024)S(1)} fusion(s32[8192]{0:T(1024)S(1)} %compare_select_fusion.1, s32[8192]{0:T(1024)S(1)} %iota.46, s32[]{:T(128)} %constant.66.clone.1), kind=kCustom, calls=%fused_computation.208 | custom fusion | bytes 32772 | tf_op jit(solution)/shard_map/scatter | solution.py:79
  75.2 50.9 %all-to-all-done = f32[2,8,128,1024]{3,2,0,1:T(8,128)} async-done(((f32[2,8,128,1024]{3,2,0,1:T(8,128)}), f32[2,8,128,1024]{3,2,0,1:T(8,128)}, u32[]{:S(2)}, u32[]{:S(2)}) %all-to-all-start) | async-done | bytes 8388640 | tf_op jit(solution)/shard_map/all_to_all | solution.py:84
  126.1 8.7 %copy.22 = f32[2,8,128,1024]{2,3,1,0:T(8,128)} copy(f32[2,8,128,1024]{3,2,0,1:T(8,128)} %all-to-all-done) | data formatting | bytes 16777216 | tf_op jit(solution)/shard_map/all_to_all | solution.py:84
  134.8 15.4 %copy.23 = f32[2,128,8192]{1,0,2:T(2,128)} copy(f32[2,128,8192]{1,2,0:T(8,128)} %bitcast.173) | data formatting | bytes 16777216 | tf_op jit(solution)/shard_map/all_to_all | solution.py:84
  150.1 59.4 %gather_fusion = f32[8192,2,128]{2,1,0:T(2,128)} fusion(f32[2,128,8192]{1,0,2:T(2,128)} %copy.23, s32[8192]{0:T(1024)S(1)} %fusion.166), kind=kCustom, calls=%fused_computation | custom fusion | bytes 16809984 | tf_op jit(solution)/shard_map/jit(_take)/gather | solution.py:83
  209.5 11.5 %gather.7 = f32[256,64,128]{0,2,1:T(8,128)} reshape(f32[2,128,8192]{1,0,2:T(2,128)} %bitcast.172) | data formatting | bytes 16777216 | tf_op jit(solution)/shard_map/jit(_take)/gather | solution.py:83
  221.0 8.7 %copy.24 = f32[256,64,128]{2,1,0:T(8,128)} copy(f32[256,64,128]{0,2,1:T(8,128)} %gather.7) | data formatting | bytes 16777216 | tf_op jit(solution)/shard_map/jit(_take)/gather | solution.py:83
  229.7 13.0 %fusion.4 = f32[256,64,128]{2,1,0:T(8,128)S(1)} fusion(f32[256,64,128]{2,1,0:T(8,128)} %copy.24, pred[64,128]{1,0:T(8,128)(4,1)S(1)} %and_bitcast_fusion), kind=kOutput, calls=%fused_computation.12 | convolution fusion | flops 3223732224 | bytes 16785408 | tf_op jit(solution)/shard_map/dot_general | solution.py:38
  242.8 8.9 %multiply_bitcast_fusion = f32[256,64,128]{2,1,0:T(8,128)S(1)} fusion(f32[256,64,128]{2,1,0:T(8,128)S(1)} %fusion.4), kind=kOutput, calls=%fused_computation.11 | convolution fusion | flops 1612800000 | bytes 16777216 | tf_op jit(solution)/shard_map/ab,nbc->nac/dot_general | solution.py:39
  253.3 5.8 fusion.20
  259.1 5.6 fusion.18
  264.7 5.6 fusion.70
  270.3 4.8 fusion.38
  275.0 5.7 fusion.73
  280.7 4.9 fusion.34
  285.6 4.6 fusion.3
  290.2 4.6 fusion.2
  296.6 134.8 %all-reduce.3.cloned.1.call-done = f32[2,32,8192]{2,1,0:T(8,128)} async-done(((f32[2,32,8192]{2,1,0:T(8,128)}), f32[2,32,8192]{2,1,0:T(8,128)}) %all-reduce.3.cloned.1.call-update) | async-done | bytes 2097168 | tf_op jit(solution)/shard_map/psum | solution.py:92
  443.9 5.6 fusion.14
  449.4 5.8 fusion.12
  455.2 5.6 fusion.76
  465.3 6.0 fusion.79
  475.9 4.8 fusion.1
  480.7 4.6 fusion
  486.8 133.5 %all-reduce.5.cloned.1.call-done = f32[2,32,8192]{2,1,0:T(8,128)} async-done(((f32[2,32,8192]{2,1,0:T(8,128)}), f32[2,32,8192]{2,1,0:T(8,128)}) %all-reduce.5.cloned.1.call-update) | async-done | bytes 2097168 | tf_op jit(solution)/shard_map/psum | solution.py:92
  632.7 5.8 fusion.8
  638.5 5.6 fusion.6
  644.3 5.8 fusion.85
  650.1 5.6 fusion.91
  656.4 38.9 %psum.23 = f32[32]{0:T(128)S(1)} all-reduce(f32[32]{0:T(128)S(1)} %get-tuple-element.5), channel_id=1, replica_groups=mesh['pix'=4,'mode'=8] {'pix','mode'}, use_global_device_ids=true, to_apply=%region_6.9 | all-reduce | flops 32 | bytes 256 | tf_op jit(solution)/shard_map/psum | solution.py:96
  (69 shorter events, 61.6 us)
Async XLA Ops:
  26.3 5.4 copy-start.7
  26.3 99.8 %all-to-all-start = ((f32[2,8,128,1024]{3,2,0,1:T(8,128)}), f32[2,8,128,1024]{3,2,0,1:T(8,128)}, u32[]{:S(2)}, u32[]{:S(2)}) async-start(f32[2,8,128,1024]{3,2,0,1:T(8,128)} %copy.21), calls=%async_computation | async-start | bytes 16777216 | tf_op jit(solution)/shard_map/all_to_all | solution.py:84
  31.6 9.7 %copy-start.8 = (s32[8192]{0:T(1024)S(1)}, s32[8192]{0:T(1024)}, u32[]{:S(2)}) copy-start(s32[8192]{0:T(1024)} %param.9) | copy-start | bytes 98308
  31.6 399.8 %all-reduce.3.cloned.1.call-start = ((), (), s32[]{:S(2)}) async-start(), calls=%async_computation.1 | async-start | bytes 4194304 | tf_op jit(solution)/shard_map/psum | solution.py:92
  31.8 1.0 copy-start.6
  253.3 27.4 %copy-start = (f32[128,64,128]{2,1,0:T(8,128)}, f32[128,64,128]{2,1,0:T(8,128)S(1)}, u32[]{:S(2)}) copy-start(f32[128,64,128]{2,1,0:T(8,128)S(1)} %get-tuple-element.9) | copy-start | bytes 12582916
  253.3 36.9 %copy-start.3 = (f32[128,64,128]{2,1,0:T(8,128)}, f32[128,64,128]{2,1,0:T(8,128)S(1)}, u32[]{:S(2)}) copy-start(f32[128,64,128]{2,1,0:T(8,128)S(1)} %get-tuple-element.10) | copy-start | bytes 12582916
  296.4 323.9 %all-reduce.5.cloned.1.call-start = ((), (), s32[]{:S(2)}) async-start(), calls=%async_computation.2 | async-start | bytes 4194304 | tf_op jit(solution)/shard_map/psum | solution.py:92
  441.6 2.2 copy-start.4
  443.9 11.4 %copy-start.1 = (f32[128,64,128]{2,1,0:T(8,128)S(1)}, f32[128,64,128]{2,1,0:T(8,128)}, u32[]{:S(2)}) copy-start(f32[128,64,128]{2,1,0:T(8,128)} %copy-done) | copy-start | bytes 12582916
  630.5 2.2 copy-start.5
  638.5 5.7 copy-start.2
Sparse Core Ops, SparseCore 0:
  296.5 134.8 all-reduce.2
  486.9 133.3 all-reduce.4
where the time goes:
time: 711 us; the launch traced here: 705 us
  waiting for transfers between devices  319 us (45%)
  local copies, waits for them, and re-layouts  146 us (21%)
  matrix products  140 us (20%)
  other arithmetic  40.2 us (6%)
  blocking collectives  38.9 us (5%)
  between operations  14.9 us (2%)
    psum x2, waiting for transfers between devices, local(): returned = lax.psum(backward(matrix, images), ('pix', 'mode'))  268 us
    gather x3, local copies, waits for them, and re-layouts, local(): jnp.take(lax.all_to_all(demodulated, 'mode', split_axis=1, concat_axis=3,...  79.6 us
    dot_general x12, matrix products, contract_last(): lax.dot_general(first_arg, second_arg, (((1,), (1,)), ((), ())), precisio...  68.3 us
    all_to_all x1, waiting for transfers between devices, local(): lax.all_to_all(demodulated, 'mode', split_axis=1, concat_axis=3, tiled=True)  50.9 us
    psum x1, blocking collectives, local(): lax.psum(local_power, ('pix', 'mode')) / (fields.shape[2] * devices)  38.9 us
    scatter x1, local copies, waits for them, and re-layouts, local(): jnp.zeros((modes_total,), jnp.int32).at[pattern_rows].set(positions)  30.7 us
    all_to_all x2, local copies, waits for them, and re-layouts, local(): lax.all_to_all(demodulated, 'mode', split_axis=1, concat_axis=3, tiled=True)  24 us
  transfers between devices with their start and end apart: 3, of which 3 were waited for; matrix products, arithmetic and copies ran while one was open for 6% of the time, Pallas kernels for 0%

commit v1 on v0

--- a/solution.py
+++ b/solution.py
@@ -70,6 +70,11 @@
 
 
 def local(frames, phase_steps, pattern_rows, probes):
+
+    def cubes_derive(x_local, which_axis, bus_axis):
+        moved = lax.psum(x_local, axis_name=which_axis)
+        return lax.psum(moved, axis_name=bus_axis)
+
     columns = frames.shape[2]
     groups = lax.axis_size("mode")
     modes_total = columns * groups
@@ -93,7 +98,7 @@
         current = orthonormal(returned)
     fields = forward(matrix, current)
     local_power = jnp.sum(fields * fields, axis=(0, 2))
-    strengths = lax.psum(local_power, ("pix", "mode")) / (fields.shape[2] * devices)
+    strengths = cubes_derive(local_power, "mode", "pix") / (fields.shape[2] * devices)
     channels = math.sqrt(modes_total) * current
     return (channels, fields, strengths)
 

time: 711 us -> 694 us (0.976)
  blocking collectives: 38.9 us -> 22.2 us
    psum x1 -> x2, blocking collectives: 38.9 us -> 22.2 us  [the longest x1 11.8 us: cubes_derive(): moved = lax.psum(x_local, axis_name=which_axis)]
where the time goes in v1:
time: 694 us; the launch traced here: 688 us
  waiting for transfers between devices  319 us (46%)
  local copies, waits for them, and re-layouts  146 us (21%)
  matrix products  140 us (20%)
  other arithmetic  40.2 us (6%)
  blocking collectives  22.2 us (3%)
  between operations  14.9 us (2%)
    psum x2, waiting for transfers between devices, local(): returned = lax.psum(backward(matrix, images), ('pix', 'mode'))  268 us
    gather x3, local copies, waits for them, and re-layouts, local(): jnp.take(lax.all_to_all(demodulated, 'mode', split_axis=1, concat_axis=3,...  79.6 us
    dot_general x12, matrix products, contract_last(): lax.dot_general(first_arg, second_arg, (((1,), (1,)), ((), ())), precisio...  68.3 us
    all_to_all x1, waiting for transfers between devices, local(): lax.all_to_all(demodulated, 'mode', split_axis=1, concat_axis=3, tiled=True)  50.9 us
    scatter x1, local copies, waits for them, and re-layouts, local(): jnp.zeros((modes_total,), jnp.int32).at[pattern_rows].set(positions)  30.7 us
    all_to_all x2, local copies, waits for them, and re-layouts, local(): lax.all_to_all(demodulated, 'mode', split_axis=1, concat_axis=3, tiled=True)  24 us
  transfers between devices with their start and end apart: 3, of which 3 were waited for; matrix products, arithmetic and copies ran while one was open for 6% of the time, Pallas kernels for 0%

profile of v1, /device:TPU:0, one launch (start us, length us, event | category | flops | bytes accessed | tf_op | source)
XLA Modules:
  0.0 687.9 jit_solution(9773399016544378169)
XLA Ops:
  8.5 12.0 %add_multiply_fusion.1 = (f32[1,1024,1024]{2,1,0:T(8,128)S(1)}, f32[1,1024,1024]{2,1,0:T(8,128)S(1)}) fusion(f32[4,1024,1024]{2,1,0:T(8,128)} %param.7, f32[]{:T(128)} %bitcast.9, f32[]{:T(128)} %bitcast.8, f32[]{:T(128)} %bitcast.7, f32[]{:T(128)} %bitcast.6, f32[]{:T(128)} %bitcast.14, f32[]{:T(128)} %bitcast.13, f32[]{:T(128)} %bitcast.12, f32[]{:T(128)} %bitcast.11), kind=kLoop, calls=%fused_computation.52 | loop fusion | flops 16777216 | bytes 25165856 | tf_op jit(solution)/shard_map/mul | solution.py:20
  26.3 5.3 all-to-all-start
  41.4 30.7 %scatter_custom_fusion = s32[8192]{0:T(1024)S(1)} fusion(s32[8192]{0:T(1024)S(1)} %compare_select_fusion.1, s32[8192]{0:T(1024)S(1)} %iota.46, s32[]{:T(128)} %constant.66.clone.1), kind=kCustom, calls=%fused_computation.208 | custom fusion | bytes 32772 | tf_op jit(solution)/shard_map/scatter | solution.py:84
  75.2 50.9 %all-to-all-done = f32[2,8,128,1024]{3,2,0,1:T(8,128)} async-done(((f32[2,8,128,1024]{3,2,0,1:T(8,128)}), f32[2,8,128,1024]{3,2,0,1:T(8,128)}, u32[]{:S(2)}, u32[]{:S(2)}) %all-to-all-start) | async-done | bytes 8388640 | tf_op jit(solution)/shard_map/all_to_all | solution.py:89
  126.1 8.7 %copy.22 = f32[2,8,128,1024]{2,3,1,0:T(8,128)} copy(f32[2,8,128,1024]{3,2,0,1:T(8,128)} %all-to-all-done) | data formatting | bytes 16777216 | tf_op jit(solution)/shard_map/all_to_all | solution.py:89
  134.8 15.4 %copy.23 = f32[2,128,8192]{1,0,2:T(2,128)} copy(f32[2,128,8192]{1,2,0:T(8,128)} %bitcast.173) | data formatting | bytes 16777216 | tf_op jit(solution)/shard_map/all_to_all | solution.py:89
  150.1 59.4 %gather_fusion = f32[8192,2,128]{2,1,0:T(2,128)} fusion(f32[2,128,8192]{1,0,2:T(2,128)} %copy.23, s32[8192]{0:T(1024)S(1)} %fusion.166), kind=kCustom, calls=%fused_computation | custom fusion | bytes 16809984 | tf_op jit(solution)/shard_map/jit(_take)/gather | solution.py:88
  209.5 11.5 %gather.7 = f32[256,64,128]{0,2,1:T(8,128)} reshape(f32[2,128,8192]{1,0,2:T(2,128)} %bitcast.172) | data formatting | bytes 16777216 | tf_op jit(solution)/shard_map/jit(_take)/gather | solution.py:88
  221.0 8.7 %copy.24 = f32[256,64,128]{2,1,0:T(8,128)} copy(f32[256,64,128]{0,2,1:T(8,128)} %gather.7) | data formatting | bytes 16777216 | tf_op jit(solution)/shard_map/jit(_take)/gather | solution.py:88
  229.7 13.0 %fusion.4 = f32[256,64,128]{2,1,0:T(8,128)S(1)} fusion(f32[256,64,128]{2,1,0:T(8,128)} %copy.24, pred[64,128]{1,0:T(8,128)(4,1)S(1)} %and_bitcast_fusion), kind=kOutput, calls=%fused_computation.12 | convolution fusion | flops 3223732224 | bytes 16785408 | tf_op jit(solution)/shard_map/dot_general | solution.py:38
  242.8 8.9 %multiply_bitcast_fusion = f32[256,64,128]{2,1,0:T(8,128)S(1)} fusion(f32[256,64,128]{2,1,0:T(8,128)S(1)} %fusion.4), kind=kOutput, calls=%fused_computation.11 | convolution fusion | flops 1612800000 | bytes 16777216 | tf_op jit(solution)/shard_map/ab,nbc->nac/dot_general | solution.py:39
  253.3 5.8 fusion.20
  259.1 5.6 fusion.18
  264.7 5.6 fusion.70
  270.3 4.8 fusion.38
  275.0 5.7 fusion.73
  280.7 4.9 fusion.34
  290.2 4.6 fusion.2
  296.6 134.8 %all-reduce.3.cloned.1.call-done = f32[2,32,8192]{2,1,0:T(8,128)} async-done(((f32[2,32,8192]{2,1,0:T(8,128)}), f32[2,32,8192]{2,1,0:T(8,128)}) %all-reduce.3.cloned.1.call-update) | async-done | bytes 2097168 | tf_op jit(solution)/shard_map/psum | solution.py:97
  443.9 5.6 fusion.14
  449.4 5.8 fusion.12
  455.2 5.6 fusion.76
  465.3 6.0 fusion.79
  475.9 4.8 fusion.1
  480.7 4.6 fusion
  486.8 133.5 %all-reduce.5.cloned.1.call-done = f32[2,32,8192]{2,1,0:T(8,128)} async-done(((f32[2,32,8192]{2,1,0:T(8,128)}), f32[2,32,8192]{2,1,0:T(8,128)}) %all-reduce.5.cloned.1.call-update) | async-done | bytes 2097168 | tf_op jit(solution)/shard_map/psum | solution.py:97
  632.7 5.8 fusion.8
  638.5 5.6 fusion.6
  644.3 5.8 fusion.85
  650.1 5.6 fusion.91
  656.4 11.8 %psum.30 = f32[32]{0:T(128)S(1)} all-reduce(f32[32]{0:T(128)S(1)} %get-tuple-element.5), channel_id=1, replica_groups=mesh['pix'=4,'mode'=8] {'mode'}, use_global_device_ids=true, to_apply=%region_6.9 | all-reduce | flops 32 | bytes 256 | tf_op jit(solution)/shard_map/psum | solution.py:75
  668.2 10.4 %psum.31 = f32[32]{0:T(128)S(1)} all-reduce(f32[32]{0:T(128)S(1)} %psum.30), channel_id=1, replica_groups=mesh['pix'=4,'mode'=8] {'pix'}, use_global_device_ids=true, to_apply=%region_7.10 | all-reduce | flops 32 | bytes 256 | tf_op jit(solution)/shard_map/psum | solution.py:76
  (70 shorter events, 66.2 us)
Async XLA Ops:
  26.3 5.4 copy-start.7
  26.3 99.8 %all-to-all-start = ((f32[2,8,128,1024]{3,2,0,1:T(8,128)}), f32[2,8,128,1024]{3,2,0,1:T(8,128)}, u32[]{:S(2)}, u32[]{:S(2)}) async-start(f32[2,8,128,1024]{3,2,0,1:T(8,128)} %copy.21), calls=%async_computation | async-start | bytes 16777216 | tf_op jit(solution)/shard_map/all_to_all | solution.py:89
  31.6 9.7 %copy-start.8 = (s32[8192]{0:T(1024)S(1)}, s32[8192]{0:T(1024)}, u32[]{:S(2)}) copy-start(s32[8192]{0:T(1024)} %param.9) | copy-start | bytes 98308
  31.6 399.8 %all-reduce.3.cloned.1.call-start = ((), (), s32[]{:S(2)}) async-start(), calls=%async_computation.1 | async-start | bytes 4194304 | tf_op jit(solution)/shard_map/psum | solution.py:97
  31.8 1.0 copy-start.6
  253.3 27.4 %copy-start = (f32[128,64,128]{2,1,0:T(8,128)}, f32[128,64,128]{2,1,0:T(8,128)S(1)}, u32[]{:S(2)}) copy-start(f32[128,64,128]{2,1,0:T(8,128)S(1)} %get-tuple-element.9) | copy-start | bytes 12582916
  253.3 36.9 %copy-start.3 = (f32[128,64,128]{2,1,0:T(8,128)}, f32[128,64,128]{2,1,0:T(8,128)S(1)}, u32[]{:S(2)}) copy-start(f32[128,64,128]{2,1,0:T(8,128)S(1)} %get-tuple-element.10) | copy-start | bytes 12582916
  296.4 323.9 %all-reduce.5.cloned.1.call-start = ((), (), s32[]{:S(2)}) async-start(), calls=%async_computation.2 | async-start | bytes 4194304 | tf_op jit(solution)/shard_map/psum | solution.py:97
  441.6 2.2 copy-start.4
  443.9 11.4 %copy-start.1 = (f32[128,64,128]{2,1,0:T(8,128)S(1)}, f32[128,64,128]{2,1,0:T(8,128)}, u32[]{:S(2)}) copy-start(f32[128,64,128]{2,1,0:T(8,128)} %copy-done) | copy-start | bytes 12582916
  630.5 2.2 copy-start.5
  638.5 5.7 copy-start.2
Sparse Core Ops, SparseCore 0:
  296.5 134.8 all-reduce.2
  486.9 133.3 all-reduce.4
